TPU v7x, 256 devices: a whole 4x4x8 slice. The times are simulated.
256 devices in a mesh: pipe: 2 (over y_hi), ctx: 16 (over y_lo, x, core), tp: 8 (over z).
Axes of the slice: x: 4, y: 4 (y_hi: 2, y_lo: 2; y = y_hi * 2 + y_lo), z: 8, core: 2. Of those that a mesh axis runs over, the one named last changes fastest.
Arguments:
- x_in: bfloat16 [2, 2048, 8192], P(None, 'ctx', 'tp'), may hold values from -6 to 6
- hidden_in: bfloat16 [2, 2048, 8192], P(None, ('ctx', 'tp')), may hold values from -6 to 6
- gate_z: bfloat16 [2, 2, 2048, 8192], P('pipe', None, 'ctx', 'tp'), may hold values from -6 to 6
- out_proj: bfloat16 [8192, 8192], P('tp', 'ctx'), may hold values from -0.0625 to 0.0625
- in_proj: bfloat16 [8192, 8192], P('tp', 'ctx'), may hold values from -0.0625 to 0.0625
- norm_gain: float32 [8192], replicated, may hold values from 0.1 to 1.9
- conv_weight: float32 [2, 4, 8192], P('pipe', None, 'tp'), may hold values from -3 to 3
- conv_bias: float32 [2, 8192], P('pipe', 'tp'), may hold values from -3 to 3
- x_proj: bfloat16 [2, 8192, 544], P('pipe', 'tp'), may hold values from -0.0625 to 0.0625
- dt_proj: bfloat16 [2, 512, 8192], P('pipe', None, 'tp'), may hold values from -0.25 to 0.25
- dt_bias: float32 [2, 8192], P('pipe', 'tp'), may hold values from -3 to -1
- decay_rate: float32 [2, 16, 8192], P('pipe', None, 'tp'), may hold values from 0.00048828125 to 1
- skip: float32 [2, 8192], P('pipe', 'tp'), may hold values from 0.1 to 1.9
Outputs:
- mixed: bfloat16 [2, 2, 2048, 8192], P('pipe', None, 'ctx', 'tp')
All inputs are finite; a program needn't handle non-finite values.
Results may differ from a plain program's by a relative error of at most 0.017.
Values may be sent and summed in bfloat16 or wider, within the bound.
No kernel may reach another device: no remote copies, remote signals or barrier semaphores. Data moves between devices by JAX's collectives and lax.ppermute only.
A program may use at most 128 MiB of HBM per device.

v0:
```python
import jax
import jax.numpy as jnp
from jax import lax
from jax.sharding import PartitionSpec as P


def shifted(block, axis, distance):
    devices = range(lax.axis_size(axis))
    route = [(i - distance, i) for i in devices if i - distance in devices]
    return lax.ppermute(block, axis, route)


def entering(part, axis, combine, identity):
    place = lax.axis_index(axis)
    gathered = jax.tree.map(lambda a: lax.all_gather(a, axis), part)
    state = jax.tree.map(lambda a, e: jnp.zeros_like(a) + jnp.asarray(e, a.dtype), part, identity)

    def one(step, state):
        return combine(
            state, jax.tree.map(lambda a: lax.dynamic_index_in_dim(a, step, 0, False), gathered)
        )

    return lax.fori_loop(0, place, one, state)


def link_pair(earlier, later):
    return (earlier[0] * later[0], earlier[1] * later[0] + later[1])


def rank_norm(rate_low):
    return (
        rate_low * lax.rsqrt(jnp.mean(rate_low * rate_low, axis=1, keepdims=True) + 1e-06)
    ).astype(jnp.bfloat16)


def sweep_state(start_state, step_size, active_wide, input_map, output_map, decay):
    count = step_size.shape[0]
    span = 8
    blocks = count // span

    def fold_block(state, rows):
        step_rows, act_rows, in_rows, out_rows = rows
        outputs = []
        for inner in range(span):
            state = (
                jnp.exp(-step_rows[inner][None, :] * decay) * state
                + in_rows[inner][:, None] * (step_rows[inner] * act_rows[inner])[None, :]
            )
            outputs.append(jnp.sum(out_rows[inner][:, None] * state, axis=0))
        return (state, jnp.stack(outputs, axis=0))

    rows = (
        step_size.reshape(blocks, span, -1),
        active_wide.reshape(blocks, span, -1),
        input_map.reshape(blocks, span, -1),
        output_map.reshape(blocks, span, -1),
    )
    final_state, outputs = lax.scan(fold_block, start_state, rows)
    return (final_state, outputs.reshape(count, -1))


def run_section(inputs, gate, conv_weight, conv_bias, x_proj, dt_proj, dt_bias, decay_rate, skip):
    count = inputs.shape[0]
    width = inputs.shape[1]
    taps_count = conv_weight.shape[1]
    rank = dt_proj.shape[1]
    nstate = decay_rate.shape[1]
    rim_rows = shifted(inputs[count - (taps_count - 1) :], "ctx", 1)
    wide_in = inputs.astype(jnp.float32)
    padded = jnp.concatenate([rim_rows.astype(jnp.float32), wide_in], axis=0)
    convolved = conv_bias[0][None, :] + jnp.zeros((count, width), jnp.float32)
    for offset in range(taps_count):
        convolved = convolved + conv_weight[0, offset][None, :] * padded[offset : offset + count]
    activated = jax.nn.silu(convolved).astype(jnp.bfloat16)
    partial_proj = jnp.dot(activated, x_proj[0], preferred_element_type=jnp.float32)
    projected = lax.psum(partial_proj, "tp")
    rate_normed = rank_norm(projected[:, :rank])
    maps = projected[:, rank:]
    step_size = jax.nn.softplus(
        jnp.dot(rate_normed, dt_proj[0], preferred_element_type=jnp.float32) + dt_bias[0][None, :]
    )
    input_map = maps[:, :nstate]
    output_map = maps[:, nstate:]
    active_wide = activated.astype(jnp.float32)
    decay = decay_rate[0]
    empty_state = jnp.zeros((nstate, width), jnp.float32)
    end_state, _ = sweep_state(empty_state, step_size, active_wide, input_map, output_map, decay)
    total_decay = jnp.exp(-decay * jnp.sum(step_size, axis=0)[None, :])
    _, incoming = entering(
        (total_decay, end_state),
        "ctx",
        link_pair,
        (jnp.ones_like(total_decay), jnp.zeros_like(end_state)),
    )
    _, state_response = sweep_state(incoming, step_size, active_wide, input_map, output_map, decay)
    response = state_response + skip[0][None, :] * active_wide
    return (response * jax.nn.silu(gate.astype(jnp.float32))).astype(jnp.bfloat16)


def shards(
    x_in,
    hidden_in,
    gate_z,
    out_proj,
    in_proj,
    norm_gain,
    conv_weight,
    conv_bias,
    x_proj,
    dt_proj,
    dt_bias,
    decay_rate,
    skip,
):
    micro = x_in.shape[0]
    segments = lax.axis_size("pipe")
    segment = lax.axis_index("pipe")
    ticks = micro + segments - 1
    own_link = jnp.where(segment == 0, out_proj, in_proj)
    link_full = lax.all_gather(own_link, "ctx", axis=1, tiled=True)
    results = jnp.zeros(gate_z.shape, jnp.bfloat16)
    received = jnp.zeros(hidden_in.shape[1:], jnp.bfloat16)
    for tick in range(ticks):
        own_rows = x_in[min(tick, micro - 1)]
        if tick == 0:
            inputs = own_rows
        else:
            wide = received.astype(jnp.float32)
            normed_share = (
                wide
                * lax.rsqrt(jnp.mean(wide * wide, axis=1, keepdims=True) + 1e-05)
                * norm_gain[None, :]
            ).astype(jnp.bfloat16)
            normed = lax.all_gather(normed_share, "tp", axis=0, tiled=True)
            from_link = lax.dot_general(
                normed, link_full, (((1,), (1,)), ((), ())), preferred_element_type=jnp.float32
            ).astype(jnp.bfloat16)
            inputs = jnp.where(segment == 0, own_rows, from_link)
        slot = tick - segment
        valid = jnp.logical_and(slot >= 0, slot < micro)
        safe_slot = jnp.clip(slot, 0, micro - 1)
        gate = lax.dynamic_index_in_dim(gate_z[0], safe_slot, 0, keepdims=False)
        mixed = run_section(
            inputs, gate, conv_weight, conv_bias, x_proj, dt_proj, dt_bias, decay_rate, skip
        )
        current = lax.dynamic_index_in_dim(results[0], safe_slot, 0, keepdims=False)
        chosen = jnp.where(valid, mixed, current)
        zero_index = jnp.zeros((), jnp.int32)
        results = lax.dynamic_update_slice(
            results, chosen[None, None], (zero_index, safe_slot, zero_index, zero_index)
        )
        if tick + 1 < ticks:
            partial_link = jnp.dot(mixed, link_full, preferred_element_type=jnp.float32)
            link_share = lax.psum_scatter(partial_link, "tp", scatter_dimension=0, tiled=True)
            carried = (hidden_in[min(tick, micro - 1)].astype(jnp.float32) + link_share).astype(
                jnp.bfloat16
            )
            received = shifted(carried, "pipe", 1)
    return results


def solution(mesh):
    in_specs = (
        P(None, "ctx", "tp"),
        P(None, ("ctx", "tp"), None),
        P("pipe", None, "ctx", "tp"),
        P("tp", "ctx"),
        P("tp", "ctx"),
        P(),
        P("pipe", None, "tp"),
        P("pipe", "tp"),
        P("pipe", "tp", None),
        P("pipe", None, "tp"),
        P("pipe", "tp"),
        P("pipe", None, "tp"),
        P("pipe", "tp"),
    )
    out_specs = P("pipe", None, "ctx", "tp")
    return jax.shard_map(shards, mesh=mesh, in_specs=in_specs, out_specs=out_specs, check_vma=False)
```

profile of v0, /device:TPU:15, one launch (start us, length us, event | category | flops | bytes accessed | tf_op | source)
XLA Modules:
  0.0 971.4 jit_solution(17711247916065645314)
XLA Ops:
  12.9 73.6 %all-reduce.4.cloned.1.call-done = f32[128,544]{0,1:T(8,128)} async-done(((f32[128,544]{0,1:T(8,128)}), f32[128,544]{0,1:T(8,128)}) %all-reduce.4.cloned.1.call-update) | async-done | bytes 278544 | tf_op jit(solution)/shard_map/psum | solution.py:76
  91.2 21.5 %while.111 = (s32[]{:T(128)}, f32[16,1024]{1,0:T(8,128)S(1)}, f32[16,8,1024]{2,1,0:T(8,128)}, f32[16,1024]{1,0:T(8,128)S(1)}, f32[16,8,16]{2,1,0:T(8,128)S(1)}, ...) while((s32[]{:T(128)}, f32[16,1024]{1,0:T(8,128)S(1)}, ...), condition=%wide.region_4.5_spmd.clone, body=%wide.region_3.4_spmd.clone.sunk | while | flops 557066 | bytes 396047 | solution.py:58
  115.4 34.2 %all-gather.25.cloned.1.call-done = f32[256,1024]{1,0:T(8,128)} async-done(((f32[16,1024]{1,0:T(8,128)}), f32[256,1024]{1,0:T(8,128)}) %all-gather.25.cloned.1.call-update) | async-done | bytes 1048592 | tf_op jit(solution)/shard_map/all_gather | solution.py:15
  149.6 36.6 %all-gather.13.cloned.1.call-done = f32[16,16,1024]{2,1,0:T(8,128)} async-done(((f32[1,16,1024]{2,1,0:T(8,128)}), f32[16,16,1024]{2,1,0:T(8,128)}) %all-gather.13.cloned.1.call-update) | async-done | bytes 1048592 | tf_op jit(solution)/shard_map/all_gather | solution.py:15
  186.1 13.9 %while.105 = (s32[]{:T(128)}, f32[16,1024]{1,0:T(8,128)S(1)}, s32[]{:T(128)}, f32[16,16,1024]{2,1,0:T(8,128)}, f32[16,16,1024]{2,1,0:T(8,128)}, /*index=5*/s32[]{:T(128)}, s32[]{:T(128)}, s32[]{:T(128)}) while((s32[]{:T(128)}, f32[16,1024]{1,0:T(8,128)S(1)}, s32[]{:T(128)}, f32[16,16,1024]{2,1,0:T(8,128)}, f32[16,16,1024]{2,1,0:T(8,128)}, ...), condition=%wide.region_6.7_spmd, body=%wide.region_5.6_spmd.sunk | while | flops 32773 | bytes 262267 | solution.py:23
  200.1 28.0 %while.106 = (s32[]{:T(128)}, f32[16,1024]{1,0:T(8,128)S(1)}, f32[16,8,1024]{2,1,0:T(8,128)S(1)}, f32[16,8,1024]{2,1,0:T(8,128)}, f32[16,1024]{1,0:T(8,128)S(1)}...) while((s32[]{:T(128)}, f32[16,1024]{1,0:T(8,128)S(1)}, ...), condition=%wide.region_16.17_spmd, body=%wide.region_7.16_spmd.sunk | while | flops 1187849 | bytes 939673 | solution.py:58
  228.5 54.1 %all-gather.15.cloned.1.call-done = bf16[1024,8192]{1,0:T(8,128)(2,1)} async-done(((bf16[1024,512]{1,0:T(8,128)(2,1)}), bf16[1024,8192]{1,0:T(8,128)(2,1)}) %all-gather.15.cloned.1.call-update) | async-done | bytes 16777232 | tf_op jit(solution)/shard_map/all_gather | solution.py:120
  282.6 10.1 %fusion.225 = f32[128,8192]{1,0:T(8,128)} fusion(bf16[128,1024]{1,0:T(8,128)(2,1)S(1)} %get-tuple-element.624, bf16[1024,8192]{1,0:T(8,128)(2,1)} %all-gather.15.cloned.1.call-done), kind=kOutput, calls=%fused_computation.522 | convolution fusion | flops 2147483648 | bytes 21233664 | tf_op jit(solution)/shard_map/dot_general | solution.py:153
  292.8 56.6 %reduce-scatter.3.cloned.1.call-done = f32[16,8192]{1,0:T(8,128)} async-done(((f32[128,8192]{1,0:T(8,128)}), f32[16,8192]{1,0:T(8,128)}) %reduce-scatter.3.cloned.1.call-update) | async-done | bytes 524304 | tf_op jit(solution)/shard_map/reduce_scatter | solution.py:154
  350.4 3.7 collective-permute-start.1
  354.2 4.9 collective-permute-done.1
  360.2 38.2 %all-gather.17.cloned.1.call-done = bf16[128,8192]{1,0:T(8,128)(2,1)} async-done(((bf16[16,8192]{1,0:T(8,128)(2,1)}), bf16[128,8192]{1,0:T(8,128)(2,1)}) %all-gather.17.cloned.1.call-update) | async-done | bytes 2097168 | tf_op jit(solution)/shard_map/all_gather | solution.py:134
  398.4 12.1 %fusion.221 = (f32[128,1024]{1,0:T(8,128)S(1)}, bf16[128,1024]{1,0:T(8,128)(2,1)S(1)}) fusion(bf16[128,8192]{1,0:T(8,128)(2,1)} %all-gather.17.cloned.1.call-done, bf16[1024,8192]{1,0:T(8,128)(2,1)} %all-gather.15.cloned.1.call-done, bf16[2,128,1024]{2,1,0:T(8,128)(2,1)S(1)} %copy-done.6, pred[]{:T(512)S(6)} %eq.2), kind=kOutput, calls=%fused_computation.518 | convolution fusion | flops 2147876864 | bytes 19922944 | tf_op jit(solution)/shard_map/dot_general | solution.py:135
  411.8 6.1 collective-permute-done.2
  419.7 69.1 %all-reduce.6.cloned.1.call-done = f32[128,544]{0,1:T(8,128)} async-done(((f32[128,544]{0,1:T(8,128)}), f32[128,544]{0,1:T(8,128)}) %all-reduce.6.cloned.1.call-update) | async-done | bytes 278544 | tf_op jit(solution)/shard_map/psum | solution.py:76
  492.6 4.5 while.112
  499.3 34.7 %all-gather.27.cloned.1.call-done = f32[256,1024]{1,0:T(8,128)} async-done(((f32[16,1024]{1,0:T(8,128)}), f32[256,1024]{1,0:T(8,128)}) %all-gather.27.cloned.1.call-update) | async-done | bytes 1048592 | tf_op jit(solution)/shard_map/all_gather | solution.py:15
  534.1 36.6 %all-gather.19.cloned.1.call-done = f32[16,16,1024]{2,1,0:T(8,128)} async-done(((f32[1,16,1024]{2,1,0:T(8,128)}), f32[16,16,1024]{2,1,0:T(8,128)}) %all-gather.19.cloned.1.call-update) | async-done | bytes 1048592 | tf_op jit(solution)/shard_map/all_gather | solution.py:15
  570.6 13.9 %while.107 = (s32[]{:T(128)}, f32[16,1024]{1,0:T(8,128)S(1)}, s32[]{:T(128)}, f32[16,16,1024]{2,1,0:T(8,128)}, f32[16,16,1024]{2,1,0:T(8,128)}, /*index=5*/s32[]{:T(128)}, s32[]{:T(128)}, s32[]{:T(128)}) while((s32[]{:T(128)}, f32[16,1024]{1,0:T(8,128)S(1)}, s32[]{:T(128)}, f32[16,16,1024]{2,1,0:T(8,128)}, f32[16,16,1024]{2,1,0:T(8,128)}, ...), condition=%wide.region_25.26_spmd, body=%wide.region_24.25_spmd.sunk | while | flops 32773 | bytes 262267 | solution.py:23
  584.6 38.5 %while.108 = (s32[]{:T(128)}, f32[16,1024]{1,0:T(8,128)S(1)}, f32[16,8,1024]{2,1,0:T(8,128)S(1)}, f32[16,8,1024]{2,1,0:T(8,128)}, f32[16,1024]{1,0:T(8,128)S(1)}...) while((s32[]{:T(128)}, f32[16,1024]{1,0:T(8,128)S(1)}, ...), condition=%wide.region_35.36_spmd, body=%wide.region_26.35_spmd.sunk | while | flops 1187849 | bytes 939673 | solution.py:58
  624.3 10.3 %fusion.226 = f32[128,8192]{1,0:T(8,128)} fusion(bf16[128,1024]{1,0:T(8,128)(2,1)S(1)} %get-tuple-element.620, bf16[1024,8192]{1,0:T(8,128)(2,1)} %all-gather.15.cloned.1.call-done), kind=kOutput, calls=%fused_computation.523 | convolution fusion | flops 2147483648 | bytes 21233664 | tf_op jit(solution)/shard_map/dot_general | solution.py:153
  634.7 55.4 %reduce-scatter.5.cloned.1.call-done = f32[16,8192]{1,0:T(8,128)} async-done(((f32[128,8192]{1,0:T(8,128)}), f32[16,8192]{1,0:T(8,128)}) %reduce-scatter.5.cloned.1.call-update) | async-done | bytes 524304 | tf_op jit(solution)/shard_map/reduce_scatter | solution.py:154
  695.0 4.9 collective-permute-done.3
  701.0 38.2 %all-gather.21.cloned.1.call-done = bf16[128,8192]{1,0:T(8,128)(2,1)} async-done(((bf16[16,8192]{1,0:T(8,128)(2,1)}), bf16[128,8192]{1,0:T(8,128)(2,1)}) %all-gather.21.cloned.1.call-update) | async-done | bytes 2097168 | tf_op jit(solution)/shard_map/all_gather | solution.py:134
  739.2 12.1 %fusion.223 = (f32[128,1024]{1,0:T(8,128)S(1)}, bf16[128,1024]{1,0:T(8,128)(2,1)S(1)}) fusion(bf16[128,8192]{1,0:T(8,128)(2,1)} %all-gather.21.cloned.1.call-done, bf16[1024,8192]{1,0:T(8,128)(2,1)} %all-gather.15.cloned.1.call-done, bf16[2,128,1024]{2,1,0:T(8,128)(2,1)S(1)} %copy-done.7, pred[]{:T(512)S(6)} %eq.2), kind=kOutput, calls=%fused_computation.520 | convolution fusion | flops 2147876864 | bytes 19922944 | tf_op jit(solution)/shard_map/dot_general | solution.py:135
  752.6 6.1 collective-permute-done.4
  760.3 69.3 %all-reduce.8.cloned.1.call-done = f32[128,544]{0,1:T(8,128)} async-done(((f32[128,544]{0,1:T(8,128)}), f32[128,544]{0,1:T(8,128)}) %all-reduce.8.cloned.1.call-update) | async-done | bytes 278544 | tf_op jit(solution)/shard_map/psum | solution.py:76
  833.3 4.6 while.113
  840.8 34.1 %all-gather.29.cloned.1.call-done = f32[256,1024]{1,0:T(8,128)} async-done(((f32[16,1024]{1,0:T(8,128)}), f32[256,1024]{1,0:T(8,128)}) %all-gather.29.cloned.1.call-update) | async-done | bytes 1048592 | tf_op jit(solution)/shard_map/all_gather | solution.py:15
  874.9 36.4 %all-gather.23.cloned.1.call-done = f32[16,16,1024]{2,1,0:T(8,128)} async-done(((f32[1,16,1024]{2,1,0:T(8,128)}), f32[16,16,1024]{2,1,0:T(8,128)}) %all-gather.23.cloned.1.call-update) | async-done | bytes 1048592 | tf_op jit(solution)/shard_map/all_gather | solution.py:15
  911.3 13.9 %while.109 = (s32[]{:T(128)}, f32[16,1024]{1,0:T(8,128)S(1)}, s32[]{:T(128)}, f32[16,16,1024]{2,1,0:T(8,128)}, f32[16,16,1024]{2,1,0:T(8,128)}, /*index=5*/s32[]{:T(128)}, s32[]{:T(128)}, s32[]{:T(128)}) while((s32[]{:T(128)}, f32[16,1024]{1,0:T(8,128)S(1)}, s32[]{:T(128)}, f32[16,16,1024]{2,1,0:T(8,128)}, f32[16,16,1024]{2,1,0:T(8,128)}, ...), condition=%wide.region_44.45_spmd, body=%wide.region_43.44_spmd.sunk | while | flops 32773 | bytes 262267 | solution.py:23
  925.3 38.6 %while.110 = (s32[]{:T(128)}, f32[16,1024]{1,0:T(8,128)S(1)}, f32[16,8,1024]{2,1,0:T(8,128)S(1)}, f32[16,8,1024]{2,1,0:T(8,128)}, f32[16,1024]{1,0:T(8,128)S(1)}...) while((s32[]{:T(128)}, f32[16,1024]{1,0:T(8,128)S(1)}, ...), condition=%wide.region_54.55_spmd, body=%wide.region_45.54_spmd.sunk | while | flops 1187849 | bytes 939673 | solution.py:58
  (803 shorter events, 214.9 us)
Async XLA Ops:
  6.5 80.0 %all-reduce.4.cloned.1.call-start = ((), (), s32[]{:S(2)}) async-start(), calls=%async_computation.2 | async-start | bytes 557056 | tf_op jit(solution)/shard_map/psum | solution.py:76
  7.4 81.0 %copy-start.20 = (f32[1,1024]{1,0:T(1,128)S(1)}, f32[1,1024]{1,0:T(1,128)}, u32[]{:S(2)}) copy-start(f32[1,1024]{1,0:T(1,128)} %param.41) | copy-start | bytes 12292
  7.4 3.2 collective-permute-start
  11.7 79.5 %copy-start.1 = (f32[1,16,1024]{2,1,0:T(8,128)S(1)}, f32[1,16,1024]{2,1,0:T(8,128)}, u32[]{:S(2)}) copy-start(f32[1,16,1024]{2,1,0:T(8,128)} %param.42) | copy-start | bytes 196612
  12.9 136.7 %all-gather.25.cloned.1.call-start = ((), (), s32[]{:S(2)}) async-start(), calls=%async_computation.13 | async-start | bytes 1114112 | tf_op jit(solution)/shard_map/all_gather | solution.py:15
  113.3 72.9 %all-gather.13.cloned.1.call-start = ((), (), s32[]{:S(2)}) async-start(), calls=%async_computation.3 | async-start | bytes 1114112 | tf_op jit(solution)/shard_map/all_gather | solution.py:15
  114.0 168.6 %all-gather.15.cloned.1.call-start = ((), (), s32[]{:S(2)}) async-start(), calls=%async_computation.4 | async-start | bytes 17825792 | tf_op jit(solution)/shard_map/all_gather | solution.py:120
  115.2 234.1 %reduce-scatter.3.cloned.1.call-start = ((), (), s32[]{:S(2)}) async-start(), calls=%async_computation.5 | async-start | bytes 4718592 | tf_op jit(solution)/shard_map/reduce_scatter | solution.py:154
  292.7 56.7 %copy-start.12 = (bf16[2,16,8192]{2,1,0:T(8,128)(2,1)S(1)}, bf16[2,16,8192]{2,1,0:T(8,128)(2,1)}, u32[]{:S(2)}) copy-start(bf16[2,16,8192]{2,1,0:T(8,128)(2,1)} %param.32) | copy-start | bytes 1572868
  292.7 66.6 %copy-start.17 = (f32[8192]{0:T(1024)S(1)}, f32[8192]{0:T(1024)}, u32[]{:S(2)}) copy-start(f32[8192]{0:T(1024)} %param.36) | copy-start | bytes 98308
  292.7 105.7 %copy-start.6 = (bf16[2,128,1024]{2,1,0:T(8,128)(2,1)S(1)}, bf16[2,128,1024]{2,1,0:T(8,128)(2,1)}, u32[]{:S(2)}) copy-start(bf16[2,128,1024]{2,1,0:T(8,128)(2,1)} %param.31) | copy-start | bytes 1572868
  292.7 105.7 %all-gather.17.cloned.1.call-start = ((), (), s32[]{:S(2)}) async-start(), calls=%async_computation.6 | async-start | bytes 2359296 | tf_op jit(solution)/shard_map/all_gather | solution.py:134
  350.4 8.7 collective-permute-start.1
  360.2 57.8 %copy-start.18 = (f32[1,1024]{1,0:T(1,128)S(1)}, f32[1,1024]{1,0:T(1,128)}, u32[]{:S(2)}) copy-start(f32[1,1024]{1,0:T(1,128)} %param.38) | copy-start | bytes 12292
  360.2 128.7 %all-reduce.6.cloned.1.call-start = ((), (), s32[]{:S(2)}) async-start(), calls=%async_computation.7 | async-start | bytes 557056 | tf_op jit(solution)/shard_map/psum | solution.py:76
  410.5 7.4 collective-permute-start.2
  419.5 114.6 %all-gather.27.cloned.1.call-start = ((), (), s32[]{:S(2)}) async-start(), calls=%async_computation.14 | async-start | bytes 1114112 | tf_op jit(solution)/shard_map/all_gather | solution.py:15
  497.8 72.9 %all-gather.19.cloned.1.call-start = ((), (), s32[]{:S(2)}) async-start(), calls=%async_computation.8 | async-start | bytes 1114112 | tf_op jit(solution)/shard_map/all_gather | solution.py:15
  498.5 191.6 %reduce-scatter.5.cloned.1.call-start = ((), (), s32[]{:S(2)}) async-start(), calls=%async_computation.9 | async-start | bytes 4718592 | tf_op jit(solution)/shard_map/reduce_scatter | solution.py:154
  624.3 215.0 %copy-start.5 = (bf16[1,2,128,1024]{3,2,1,0:T(8,128)(2,1)}, bf16[1,2,128,1024]{3,2,1,0:T(8,128)(2,1)S(1)}, u32[]{:S(2)}) copy-start(bf16[1,2,128,1024]{3,2,1,0:T(8,128)(2,1)S(1)} %get-tuple-element.619) | copy-start | bytes 1572868
  634.6 55.5 %copy-start.13 = (bf16[2,16,8192]{2,1,0:T(8,128)(2,1)S(1)}, bf16[2,16,8192]{2,1,0:T(8,128)(2,1)}, u32[]{:S(2)}) copy-start(bf16[2,16,8192]{2,1,0:T(8,128)(2,1)} %param.32) | copy-start | bytes 1572868
  634.6 104.5 %copy-start.7 = (bf16[2,128,1024]{2,1,0:T(8,128)(2,1)S(1)}, bf16[2,128,1024]{2,1,0:T(8,128)(2,1)}, u32[]{:S(2)}) copy-start(bf16[2,128,1024]{2,1,0:T(8,128)(2,1)} %param.31) | copy-start | bytes 1572868
  634.6 104.5 %all-gather.21.cloned.1.call-start = ((), (), s32[]{:S(2)}) async-start(), calls=%async_computation.10 | async-start | bytes 2359296 | tf_op jit(solution)/shard_map/all_gather | solution.py:134
  691.2 8.6 collective-permute-start.3
  700.9 128.7 %all-reduce.8.cloned.1.call-start = ((), (), s32[]{:S(2)}) async-start(), calls=%async_computation.11 | async-start | bytes 557056 | tf_op jit(solution)/shard_map/psum | solution.py:76
  751.3 7.4 collective-permute-start.4
  760.3 114.6 %all-gather.29.cloned.1.call-start = ((), (), s32[]{:S(2)}) async-start(), calls=%async_computation.15 | async-start | bytes 1114112 | tf_op jit(solution)/shard_map/all_gather | solution.py:15
  837.9 87.3 %copy-start.14 = (f32[16,8,1024]{2,1,0:T(8,128)}, f32[16,8,1024]{2,1,0:T(8,128)S(1)}, u32[]{:S(2)}) copy-start(f32[16,8,1024]{2,1,0:T(8,128)S(1)} %get-tuple-element.2006) | copy-start | bytes 1572868
  837.9 87.3 %copy-start.16 = (f32[16,8,16]{2,1,0:T(8,128)}, f32[16,8,16]{2,1,0:T(8,128)S(1)}, u32[]{:S(2)}) copy-start(f32[16,8,16]{2,1,0:T(8,128)S(1)} %get-tuple-element.2009) | copy-start | bytes 24580
  838.6 72.7 %all-gather.23.cloned.1.call-start = ((), (), s32[]{:S(2)}) async-start(), calls=%async_computation.12 | async-start | bytes 1114112 | tf_op jit(solution)/shard_map/all_gather | solution.py:15
  925.3 38.6 %copy-start.9 = (bf16[1,2,128,1024]{3,2,1,0:T(8,128)(2,1)S(1)}, bf16[1,2,128,1024]{3,2,1,0:T(8,128)(2,1)}, u32[]{:S(2)}) copy-start(bf16[1,2,128,1024]{3,2,1,0:T(8,128)(2,1)} %param.33) | copy-start | bytes 1572868
  925.3 38.6 %copy-start.11 = (bf16[1,1,128,1024]{3,2,1,0:T(8,128)(2,1)S(1)}, bf16[1,1,128,1024]{3,2,1,0:T(8,128)(2,1)}, u32[]{:S(2)}) copy-start(bf16[1,1,128,1024]{3,2,1,0:T(8,128)(2,1)} %constant_dynamic-slice_fusion.105) | copy-start | bytes 786436
  (8 other events, 90.3 us)
Sparse Core Ops, SparseCore 0:
  13.0 73.4 all-reduce.3
  113.4 36.1 all-gather.24
  151.4 34.6 all-gather.12
  187.8 94.7 all-gather.14
  292.8 56.4 reduce-scatter.2
  360.3 38.0 all-gather.16
  419.6 69.1 all-reduce.5
  497.9 36.1 all-gather.26
  535.9 34.6 all-gather.18
  634.7 55.3 reduce-scatter.4
  701.0 38.0 all-gather.20
  760.4 69.1 all-reduce.7
  838.7 36.1 all-gather.28
  876.6 34.6 all-gather.22
where the time goes:
time: 981 us; the launch traced here: 971 us
  waiting for transfers between devices  689 us (70%)
  other arithmetic  160 us (16%)
  matrix products  54.6 us (6%)
  local copies, waits for them, and re-layouts  35.9 us (4%)
  between operations  13.8 us (1%)
  starting transfers between devices  12.1 us (1%)
    all_gather x6, waiting for transfers between devices, entering(): gathered = jax.tree.map(lambda a: lax.all_gather(a, axis), part)  213 us
    psum x3, waiting for transfers between devices, run_section(): projected = lax.psum(partial_proj, 'tp')  212 us
    reduce_scatter x2, waiting for transfers between devices, shards(): lax.psum_scatter(partial_link, 'tp', scatter_dimension=0, tiled=True)  112 us
    all_gather x2, waiting for transfers between devices, shards(): normed = lax.all_gather(normed_share, 'tp', axis=0, tiled=True)  76.4 us
    mul x96, other arithmetic, fold_block(): step_rows[inner] * act_rows[inner]  75.6 us
    all_gather x1, waiting for transfers between devices, shards(): link_full = lax.all_gather(own_link, 'ctx', axis=1, tiled=True)  54.1 us
    add x45, other arithmetic, link_pair(): return (earlier[0] * later[0], earlier[1] * later[0] + later[1])  40.7 us
    dot_general x2, matrix products, shards(): lax.dot_general(normed, link_full, (((1,), (1,)), ((), ())), preferred_el...  24.2 us
  transfers between devices with their start and end apart: 19, of which 19 were waited for; matrix products, arithmetic and copies ran while one was open for 5% of the time, Pallas kernels for 0%

commit v1 on v0

--- a/solution.py
+++ b/solution.py
@@ -73,7 +73,7 @@
         convolved = convolved + conv_weight[0, offset][None, :] * padded[offset : offset + count]
     activated = jax.nn.silu(convolved).astype(jnp.bfloat16)
     partial_proj = jnp.dot(activated, x_proj[0], preferred_element_type=jnp.float32)
-    projected = lax.psum(partial_proj, "tp")
+    projected = jnp.sum(lax.all_gather(partial_proj, "tp"), axis=0)
     rate_normed = rank_norm(projected[:, :rank])
     maps = projected[:, rank:]
     step_size = jax.nn.softplus(

time: 981 us -> 938 us (0.956)
  waiting for transfers between devices: 689 us -> 618 us
  other arithmetic: 160 us -> 194 us
    psum x3 -> x0, waiting for transfers between devices: 212 us -> none  [run_section(): projected = lax.psum(partial_proj, 'tp')]
    all_gather x0 -> x3, waiting for transfers between devices: none -> 136 us  [run_section(): projected = jnp.sum(lax.all_gather(partial_proj, 'tp'), axis=0)]
    mul x96, other arithmetic: 75.6 us -> 110 us  [fold_block(): step_rows[inner] * act_rows[inner]]
    dynamic_slice x96, local copies, waits for them, and re-layouts: 22.7 us -> 11.8 us  [sweep_state(): final_state, outputs = lax.scan(fold_block, start_state, rows)]
where the time goes in v1:
time: 938 us; the launch traced here: 926 us
  waiting for transfers between devices  618 us (66%)
  other arithmetic  194 us (21%)
  matrix products  53.4 us (6%)
  local copies, waits for them, and re-layouts  29 us (3%)
  between operations  13.8 us (1%)
  starting transfers between devices  12.3 us (1%)
    all_gather x6, waiting for transfers between devices, entering(): gathered = jax.tree.map(lambda a: lax.all_gather(a, axis), part)  217 us
    all_gather x3, waiting for transfers between devices, run_section(): projected = jnp.sum(lax.all_gather(partial_proj, 'tp'), axis=0)  136 us
    reduce_scatter x2, waiting for transfers between devices, shards(): lax.psum_scatter(partial_link, 'tp', scatter_dimension=0, tiled=True)  112 us
    mul x96, other arithmetic, fold_block(): step_rows[inner] * act_rows[inner]  110 us
    all_gather x2, waiting for transfers between devices, shards(): normed = lax.all_gather(normed_share, 'tp', axis=0, tiled=True)  76.4 us
    all_gather x1, waiting for transfers between devices, shards(): link_full = lax.all_gather(own_link, 'ctx', axis=1, tiled=True)  54.1 us
    add x45, other arithmetic, link_pair(): return (earlier[0] * later[0], earlier[1] * later[0] + later[1])  40.7 us
    dot_general x2, matrix products, shards(): lax.dot_general(normed, link_full, (((1,), (1,)), ((), ())), preferred_el...  24.2 us
  transfers between devices with their start and end apart: 19, of which 19 were waited for; matrix products, arithmetic and copies ran while one was open for 5% of the time, Pallas kernels for 0%

profile of v1, /device:TPU:15, one launch (start us, length us, event | category | flops | bytes accessed | tf_op | source)
XLA Modules:
  0.0 925.7 jit_solution(17749491621090917880)
XLA Ops:
  12.9 48.4 %all-gather.31.cloned.1.call-done = f32[1024,544]{0,1:T(8,128)} async-done(((f32[128,544]{0,1:T(8,128)}), f32[1024,544]{0,1:T(8,128)}) %all-gather.31.cloned.1.call-update) | async-done | bytes 2228240 | tf_op jit(solution)/shard_map/all_gather | solution.py:76
  67.0 21.5 %while.111 = (s32[]{:T(128)}, f32[16,1024]{1,0:T(8,128)S(1)}, f32[16,8,1024]{2,1,0:T(8,128)}, f32[16,1024]{1,0:T(8,128)S(1)}, f32[16,8,16]{2,1,0:T(8,128)S(1)}, ...) while((s32[]{:T(128)}, f32[16,1024]{1,0:T(8,128)S(1)}, ...), condition=%wide.region_4.5_spmd.clone, body=%wide.region_3.4_spmd.clone.sunk | while | flops 557066 | bytes 396047 | solution.py:58
  91.1 35.2 %all-gather.33.cloned.1.call-done = f32[256,1024]{1,0:T(8,128)} async-done(((f32[16,1024]{1,0:T(8,128)}), f32[256,1024]{1,0:T(8,128)}) %all-gather.33.cloned.1.call-update) | async-done | bytes 1048592 | tf_op jit(solution)/shard_map/all_gather | solution.py:15
  126.3 36.6 %all-gather.19.cloned.1.call-done = f32[16,16,1024]{2,1,0:T(8,128)} async-done(((f32[1,16,1024]{2,1,0:T(8,128)}), f32[16,16,1024]{2,1,0:T(8,128)}) %all-gather.19.cloned.1.call-update) | async-done | bytes 1048592 | tf_op jit(solution)/shard_map/all_gather | solution.py:15
  162.9 13.9 %while.105 = (s32[]{:T(128)}, f32[16,1024]{1,0:T(8,128)S(1)}, s32[]{:T(128)}, f32[16,16,1024]{2,1,0:T(8,128)}, f32[16,16,1024]{2,1,0:T(8,128)}, /*index=5*/s32[]{:T(128)}, s32[]{:T(128)}, s32[]{:T(128)}) while((s32[]{:T(128)}, f32[16,1024]{1,0:T(8,128)S(1)}, s32[]{:T(128)}, f32[16,16,1024]{2,1,0:T(8,128)}, f32[16,16,1024]{2,1,0:T(8,128)}, ...), condition=%wide.region_6.7_spmd, body=%wide.region_5.6_spmd.sunk | while | flops 32773 | bytes 262267 | solution.py:23
  176.9 28.0 %while.106 = (s32[]{:T(128)}, f32[16,1024]{1,0:T(8,128)S(1)}, f32[16,8,1024]{2,1,0:T(8,128)S(1)}, f32[16,8,1024]{2,1,0:T(8,128)}, f32[16,1024]{1,0:T(8,128)S(1)}...) while((s32[]{:T(128)}, f32[16,1024]{1,0:T(8,128)S(1)}, ...), condition=%wide.region_16.17_spmd, body=%wide.region_7.16_spmd.sunk | while | flops 1187849 | bytes 939673 | solution.py:58
  205.3 54.1 %all-gather.21.cloned.1.call-done = bf16[1024,8192]{1,0:T(8,128)(2,1)} async-done(((bf16[1024,512]{1,0:T(8,128)(2,1)}), bf16[1024,8192]{1,0:T(8,128)(2,1)}) %all-gather.21.cloned.1.call-update) | async-done | bytes 16777232 | tf_op jit(solution)/shard_map/all_gather | solution.py:120
  259.4 10.1 %fusion.225 = f32[128,8192]{1,0:T(8,128)} fusion(bf16[128,1024]{1,0:T(8,128)(2,1)S(1)} %get-tuple-element.624, bf16[1024,8192]{1,0:T(8,128)(2,1)} %all-gather.21.cloned.1.call-done), kind=kOutput, calls=%fused_computation.525 | convolution fusion | flops 2147483648 | bytes 21233664 | tf_op jit(solution)/shard_map/dot_general | solution.py:153
  269.5 56.6 %reduce-scatter.3.cloned.1.call-done = f32[16,8192]{1,0:T(8,128)} async-done(((f32[128,8192]{1,0:T(8,128)}), f32[16,8192]{1,0:T(8,128)}) %reduce-scatter.3.cloned.1.call-update) | async-done | bytes 524304 | tf_op jit(solution)/shard_map/reduce_scatter | solution.py:154
  327.2 3.7 collective-permute-start.1
  331.0 4.9 collective-permute-done.1
  337.0 38.2 %all-gather.23.cloned.1.call-done = bf16[128,8192]{1,0:T(8,128)(2,1)} async-done(((bf16[16,8192]{1,0:T(8,128)(2,1)}), bf16[128,8192]{1,0:T(8,128)(2,1)}) %all-gather.23.cloned.1.call-update) | async-done | bytes 2097168 | tf_op jit(solution)/shard_map/all_gather | solution.py:134
  375.2 12.1 %fusion.221 = (f32[128,1024]{1,0:T(8,128)S(1)}, bf16[128,1024]{1,0:T(8,128)(2,1)S(1)}) fusion(bf16[128,8192]{1,0:T(8,128)(2,1)} %all-gather.23.cloned.1.call-done, bf16[1024,8192]{1,0:T(8,128)(2,1)} %all-gather.21.cloned.1.call-done, bf16[2,128,1024]{2,1,0:T(8,128)(2,1)S(1)} %copy-done.6, pred[]{:T(512)S(6)} %eq.2), kind=kOutput, calls=%fused_computation.521 | convolution fusion | flops 2147876864 | bytes 19922944 | tf_op jit(solution)/shard_map/dot_general | solution.py:135
  388.8 6.0 collective-permute-done.2
  396.3 44.1 %all-gather.35.cloned.1.call-done = f32[1024,544]{0,1:T(8,128)} async-done(((f32[128,544]{0,1:T(8,128)}), f32[1024,544]{0,1:T(8,128)}) %all-gather.35.cloned.1.call-update) | async-done | bytes 2228240 | tf_op jit(solution)/shard_map/all_gather | solution.py:76
  445.3 21.5 %while.112 = (s32[]{:T(128)}, f32[16,1024]{1,0:T(8,128)S(1)}, f32[16,8,1024]{2,1,0:T(8,128)}, f32[16,1024]{1,0:T(8,128)S(1)}, f32[16,8,16]{2,1,0:T(8,128)S(1)}, ...) while((s32[]{:T(128)}, f32[16,1024]{1,0:T(8,128)S(1)}, ...), condition=%wide.region_23.24_spmd.clone, body=%wide.region_22.23_spmd.clone.sunk | while | flops 557066 | bytes 396047 | solution.py:58
  469.0 35.8 %all-gather.37.cloned.1.call-done = f32[256,1024]{1,0:T(8,128)} async-done(((f32[16,1024]{1,0:T(8,128)}), f32[256,1024]{1,0:T(8,128)}) %all-gather.37.cloned.1.call-update) | async-done | bytes 1048592 | tf_op jit(solution)/shard_map/all_gather | solution.py:15
  504.7 36.6 %all-gather.25.cloned.1.call-done = f32[16,16,1024]{2,1,0:T(8,128)} async-done(((f32[1,16,1024]{2,1,0:T(8,128)}), f32[16,16,1024]{2,1,0:T(8,128)}) %all-gather.25.cloned.1.call-update) | async-done | bytes 1048592 | tf_op jit(solution)/shard_map/all_gather | solution.py:15
  541.3 13.9 %while.107 = (s32[]{:T(128)}, f32[16,1024]{1,0:T(8,128)S(1)}, s32[]{:T(128)}, f32[16,16,1024]{2,1,0:T(8,128)}, f32[16,16,1024]{2,1,0:T(8,128)}, /*index=5*/s32[]{:T(128)}, s32[]{:T(128)}, s32[]{:T(128)}) while((s32[]{:T(128)}, f32[16,1024]{1,0:T(8,128)S(1)}, s32[]{:T(128)}, f32[16,16,1024]{2,1,0:T(8,128)}, f32[16,16,1024]{2,1,0:T(8,128)}, ...), condition=%wide.region_25.26_spmd, body=%wide.region_24.25_spmd.sunk | while | flops 32773 | bytes 262267 | solution.py:23
  555.3 38.5 %while.108 = (s32[]{:T(128)}, f32[16,1024]{1,0:T(8,128)S(1)}, f32[16,8,1024]{2,1,0:T(8,128)S(1)}, f32[16,8,1024]{2,1,0:T(8,128)}, f32[16,1024]{1,0:T(8,128)S(1)}...) while((s32[]{:T(128)}, f32[16,1024]{1,0:T(8,128)S(1)}, ...), condition=%wide.region_35.36_spmd, body=%wide.region_26.35_spmd.sunk | while | flops 1187849 | bytes 939673 | solution.py:58
  595.0 10.2 %fusion.226 = f32[128,8192]{1,0:T(8,128)} fusion(bf16[128,1024]{1,0:T(8,128)(2,1)S(1)} %get-tuple-element.620, bf16[1024,8192]{1,0:T(8,128)(2,1)} %all-gather.21.cloned.1.call-done), kind=kOutput, calls=%fused_computation.526 | convolution fusion | flops 2147483648 | bytes 21233664 | tf_op jit(solution)/shard_map/dot_general | solution.py:153
  605.3 55.4 %reduce-scatter.5.cloned.1.call-done = f32[16,8192]{1,0:T(8,128)} async-done(((f32[128,8192]{1,0:T(8,128)}), f32[16,8192]{1,0:T(8,128)}) %reduce-scatter.5.cloned.1.call-update) | async-done | bytes 524304 | tf_op jit(solution)/shard_map/reduce_scatter | solution.py:154
  665.6 4.9 collective-permute-done.3
  671.6 38.2 %all-gather.27.cloned.1.call-done = bf16[128,8192]{1,0:T(8,128)(2,1)} async-done(((bf16[16,8192]{1,0:T(8,128)(2,1)}), bf16[128,8192]{1,0:T(8,128)(2,1)}) %all-gather.27.cloned.1.call-update) | async-done | bytes 2097168 | tf_op jit(solution)/shard_map/all_gather | solution.py:134
  709.8 12.1 %fusion.223 = (f32[128,1024]{1,0:T(8,128)S(1)}, bf16[128,1024]{1,0:T(8,128)(2,1)S(1)}) fusion(bf16[128,8192]{1,0:T(8,128)(2,1)} %all-gather.27.cloned.1.call-done, bf16[1024,8192]{1,0:T(8,128)(2,1)} %all-gather.21.cloned.1.call-done, bf16[2,128,1024]{2,1,0:T(8,128)(2,1)S(1)} %copy-done.7, pred[]{:T(512)S(6)} %eq.2), kind=kOutput, calls=%fused_computation.523 | convolution fusion | flops 2147876864 | bytes 19922944 | tf_op jit(solution)/shard_map/dot_general | solution.py:135
  723.2 6.1 collective-permute-done.4
  731.2 43.9 %all-gather.39.cloned.1.call-done = f32[1024,544]{0,1:T(8,128)} async-done(((f32[128,544]{0,1:T(8,128)}), f32[1024,544]{0,1:T(8,128)}) %all-gather.39.cloned.1.call-update) | async-done | bytes 2228240 | tf_op jit(solution)/shard_map/all_gather | solution.py:76
  780.0 21.7 %while.113 = (s32[]{:T(128)}, f32[16,1024]{1,0:T(8,128)S(1)}, f32[16,8,1024]{2,1,0:T(8,128)}, f32[16,1024]{1,0:T(8,128)S(1)}, f32[16,8,16]{2,1,0:T(8,128)S(1)}, ...) while((s32[]{:T(128)}, f32[16,1024]{1,0:T(8,128)S(1)}, ...), condition=%wide.region_42.43_spmd.clone, body=%wide.region_41.42_spmd.clone.sunk | while | flops 557066 | bytes 396047 | solution.py:58
  803.2 36.4 %all-gather.41.cloned.1.call-done = f32[256,1024]{1,0:T(8,128)} async-done(((f32[16,1024]{1,0:T(8,128)}), f32[256,1024]{1,0:T(8,128)}) %all-gather.41.cloned.1.call-update) | async-done | bytes 1048592 | tf_op jit(solution)/shard_map/all_gather | solution.py:15
  839.6 36.4 %all-gather.29.cloned.1.call-done = f32[16,16,1024]{2,1,0:T(8,128)} async-done(((f32[1,16,1024]{2,1,0:T(8,128)}), f32[16,16,1024]{2,1,0:T(8,128)}) %all-gather.29.cloned.1.call-update) | async-done | bytes 1048592 | tf_op jit(solution)/shard_map/all_gather | solution.py:15
  876.0 13.9 %while.109 = (s32[]{:T(128)}, f32[16,1024]{1,0:T(8,128)S(1)}, s32[]{:T(128)}, f32[16,16,1024]{2,1,0:T(8,128)}, f32[16,16,1024]{2,1,0:T(8,128)}, /*index=5*/s32[]{:T(128)}, s32[]{:T(128)}, s32[]{:T(128)}) while((s32[]{:T(128)}, f32[16,1024]{1,0:T(8,128)S(1)}, s32[]{:T(128)}, f32[16,16,1024]{2,1,0:T(8,128)}, f32[16,16,1024]{2,1,0:T(8,128)}, ...), condition=%wide.region_44.45_spmd, body=%wide.region_43.44_spmd.sunk | while | flops 32773 | bytes 262267 | solution.py:23
  890.0 28.2 %while.110 = (s32[]{:T(128)}, f32[16,1024]{1,0:T(8,128)S(1)}, f32[16,8,1024]{2,1,0:T(8,128)S(1)}, f32[16,8,1024]{2,1,0:T(8,128)}, f32[16,1024]{1,0:T(8,128)S(1)}...) while((s32[]{:T(128)}, f32[16,1024]{1,0:T(8,128)S(1)}, ...), condition=%wide.region_54.55_spmd, body=%wide.region_45.54_spmd.sunk | while | flops 1187849 | bytes 939673 | solution.py:58
  (805 shorter events, 240.3 us)
Async XLA Ops:
  6.5 5.1 copy-start
  6.5 54.8 %all-gather.31.cloned.1.call-start = ((), (), s32[]{:S(2)}) async-start(), calls=%async_computation.10 | async-start | bytes 2506752 | tf_op jit(solution)/shard_map/all_gather | solution.py:76
  7.4 3.2 collective-permute-start
  12.8 113.5 %all-gather.33.cloned.1.call-start = ((), (), s32[]{:S(2)}) async-start(), calls=%async_computation.11 | async-start | bytes 1114112 | tf_op jit(solution)/shard_map/all_gather | solution.py:15
  63.4 3.5 copy-start.1
  64.2 25.6 %copy-start.10 = (bf16[1024,512]{1,0:T(8,128)(2,1)S(1)}, bf16[1024,512]{1,0:T(8,128)(2,1)}, u32[]{:S(2)}) copy-start(bf16[1024,512]{1,0:T(8,128)(2,1)} %param.34) | copy-start | bytes 3145732
  89.0 73.9 %all-gather.19.cloned.1.call-start = ((), (), s32[]{:S(2)}) async-start(), calls=%async_computation.2 | async-start | bytes 1114112 | tf_op jit(solution)/shard_map/all_gather | solution.py:15
  89.8 169.6 %all-gather.21.cloned.1.call-start = ((), (), s32[]{:S(2)}) async-start(), calls=%async_computation.3 | async-start | bytes 17825792 | tf_op jit(solution)/shard_map/all_gather | solution.py:120
  91.0 235.1 %reduce-scatter.3.cloned.1.call-start = ((), (), s32[]{:S(2)}) async-start(), calls=%async_computation.4 | async-start | bytes 4718592 | tf_op jit(solution)/shard_map/reduce_scatter | solution.py:154
  176.9 28.1 %copy-start.8 = (bf16[1,2,128,1024]{3,2,1,0:T(8,128)(2,1)S(1)}, bf16[1,2,128,1024]{3,2,1,0:T(8,128)(2,1)}, u32[]{:S(2)}) copy-start(bf16[1,2,128,1024]{3,2,1,0:T(8,128)(2,1)} %param.33) | copy-start | bytes 1572868
  176.9 28.1 %copy-start.15 = (f32[1,1024]{1,0:T(1,128)S(1)}, f32[1,1024]{1,0:T(1,128)}, u32[]{:S(2)}) copy-start(f32[1,1024]{1,0:T(1,128)} %param.43) | copy-start | bytes 12292
  269.5 56.7 %copy-start.11 = (bf16[2,16,8192]{2,1,0:T(8,128)(2,1)S(1)}, bf16[2,16,8192]{2,1,0:T(8,128)(2,1)}, u32[]{:S(2)}) copy-start(bf16[2,16,8192]{2,1,0:T(8,128)(2,1)} %param.32) | copy-start | bytes 1572868
  269.5 66.6 %copy-start.13 = (f32[8192]{0:T(1024)S(1)}, f32[8192]{0:T(1024)}, u32[]{:S(2)}) copy-start(f32[8192]{0:T(1024)} %param.36) | copy-start | bytes 98308
  269.5 105.7 %copy-start.6 = (bf16[2,128,1024]{2,1,0:T(8,128)(2,1)S(1)}, bf16[2,128,1024]{2,1,0:T(8,128)(2,1)}, u32[]{:S(2)}) copy-start(bf16[2,128,1024]{2,1,0:T(8,128)(2,1)} %param.31) | copy-start | bytes 1572868
  269.5 105.7 %all-gather.23.cloned.1.call-start = ((), (), s32[]{:S(2)}) async-start(), calls=%async_computation.5 | async-start | bytes 2359296 | tf_op jit(solution)/shard_map/all_gather | solution.py:134
  327.2 8.7 collective-permute-start.1
  336.9 57.8 %copy-start.14 = (f32[1,1024]{1,0:T(1,128)S(1)}, f32[1,1024]{1,0:T(1,128)}, u32[]{:S(2)}) copy-start(f32[1,1024]{1,0:T(1,128)} %param.38) | copy-start | bytes 12292
  336.9 103.5 %all-gather.35.cloned.1.call-start = ((), (), s32[]{:S(2)}) async-start(), calls=%async_computation.12 | async-start | bytes 2506752 | tf_op jit(solution)/shard_map/all_gather | solution.py:76
  387.3 7.4 collective-permute-start.2
  396.3 108.5 %all-gather.37.cloned.1.call-start = ((), (), s32[]{:S(2)}) async-start(), calls=%async_computation.13 | async-start | bytes 1114112 | tf_op jit(solution)/shard_map/all_gather | solution.py:15
  467.5 73.9 %all-gather.25.cloned.1.call-start = ((), (), s32[]{:S(2)}) async-start(), calls=%async_computation.6 | async-start | bytes 1114112 | tf_op jit(solution)/shard_map/all_gather | solution.py:15
  468.2 192.6 %reduce-scatter.5.cloned.1.call-start = ((), (), s32[]{:S(2)}) async-start(), calls=%async_computation.7 | async-start | bytes 4718592 | tf_op jit(solution)/shard_map/reduce_scatter | solution.py:154
  595.0 208.0 %copy-start.5 = (bf16[1,2,128,1024]{3,2,1,0:T(8,128)(2,1)}, bf16[1,2,128,1024]{3,2,1,0:T(8,128)(2,1)S(1)}, u32[]{:S(2)}) copy-start(bf16[1,2,128,1024]{3,2,1,0:T(8,128)(2,1)S(1)} %get-tuple-element.619) | copy-start | bytes 1572868
  605.2 55.5 %copy-start.12 = (bf16[2,16,8192]{2,1,0:T(8,128)(2,1)S(1)}, bf16[2,16,8192]{2,1,0:T(8,128)(2,1)}, u32[]{:S(2)}) copy-start(bf16[2,16,8192]{2,1,0:T(8,128)(2,1)} %param.32) | copy-start | bytes 1572868
  605.3 104.6 %copy-start.7 = (bf16[2,128,1024]{2,1,0:T(8,128)(2,1)S(1)}, bf16[2,128,1024]{2,1,0:T(8,128)(2,1)}, u32[]{:S(2)}) copy-start(bf16[2,128,1024]{2,1,0:T(8,128)(2,1)} %param.31) | copy-start | bytes 1572868
  605.3 104.5 %all-gather.27.cloned.1.call-start = ((), (), s32[]{:S(2)}) async-start(), calls=%async_computation.8 | async-start | bytes 2359296 | tf_op jit(solution)/shard_map/all_gather | solution.py:134
  661.9 8.6 collective-permute-start.3
  671.6 103.6 %all-gather.39.cloned.1.call-start = ((), (), s32[]{:S(2)}) async-start(), calls=%async_computation.14 | async-start | bytes 2506752 | tf_op jit(solution)/shard_map/all_gather | solution.py:76
  721.9 7.4 collective-permute-start.4
  730.9 108.7 %all-gather.41.cloned.1.call-start = ((), (), s32[]{:S(2)}) async-start(), calls=%async_computation.15 | async-start | bytes 1114112 | tf_op jit(solution)/shard_map/all_gather | solution.py:15
  802.3 73.7 %all-gather.29.cloned.1.call-start = ((), (), s32[]{:S(2)}) async-start(), calls=%async_computation.9 | async-start | bytes 1114112 | tf_op jit(solution)/shard_map/all_gather | solution.py:15
  890.0 28.2 %copy-start.9 = (bf16[1,2,128,1024]{3,2,1,0:T(8,128)(2,1)S(1)}, bf16[1,2,128,1024]{3,2,1,0:T(8,128)(2,1)}, u32[]{:S(2)}) copy-start(bf16[1,2,128,1024]{3,2,1,0:T(8,128)(2,1)} %param.33) | copy-start | bytes 1572868
  (6 other events, 5.1 us)
Sparse Core Ops, SparseCore 0:
  13.0 48.2 all-gather.30
  89.2 37.1 all-gather.32
  128.2 34.6 all-gather.18
  164.6 94.7 all-gather.20
  269.6 56.4 reduce-scatter.2
  337.0 38.0 all-gather.22
  396.4 44.0 all-gather.34
  467.6 37.1 all-gather.36
  506.6 34.6 all-gather.24
  605.4 55.3 reduce-scatter.4
  671.7 38.0 all-gather.26
  731.0 44.0 all-gather.38
  802.4 37.1 all-gather.40
  841.3 34.6 all-gather.28
